TPU v7x, 32 devices: a whole 2x2x4 slice. The times are simulated.
32 devices in a mesh: kz: 4 (over x, core), en: 2 (over y), sp: 4 (over z).
Axes of the slice: x: 2, y: 2, z: 4, core: 2. Of those that a mesh axis runs over, the one named last changes fastest.
Arguments:
- green: float32 [4, 4, 4, 2, 256, 256], P('kz', 'en', 'sp'), may hold values from -0.1 to 0.1
- coupling: float32 [4, 3, 256, 256], P('sp'), may hold values from -0.375 to 0.375
- phonon_weight: float32 [3], replicated, may hold values from 0.2 to 0.6
- mode_index: int32 [4, 5], P('kz'), may hold values from 0 to 2
- onsite: float32 [4, 256], P('sp'), may hold values from 0.8 to 1.2
- hopping: float32 [4, 256], P('sp'), may hold values from 0.45 to 0.95
- energies: float32 [4], P('en'), may hold values from -0.1 to 0.1
- guess_scale: float32 [4, 4, 4], P('kz', 'en', 'sp'), may hold values from 0.45 to 0.75
Outputs:
- boundary: float32 [4, 4, 4, 2, 256, 256], P('kz', 'en', 'sp')
All inputs are finite; a program needn't handle non-finite values.
Results may differ from a plain program's by a relative error of at most 0.0003.
Values sent between devices are 32-bit elements; how exact they have to be, the bound alone decides.
A program may use at most 64 MiB of HBM per device.

v0:
```python
import functools

import jax
import jax.numpy as jnp
from jax import lax
from jax.experimental import pallas as pl
from jax.experimental.pallas import tpu as pltpu
from jax.sharding import PartitionSpec as P

REACH = 2
ROW_BLOCKS = 8
SHARES = 2
PACE = 2
WAITING = 2
MESH = pl.DeviceIdType.MESH

SIBLING, BACK, PASSED, AHEAD = range(4)


def split(value):
    high = value.astype(jnp.bfloat16)
    return high, (value - high.astype(jnp.float32)).astype(jnp.bfloat16)


def dot_split(first, second):
    left = jnp.concatenate([first[0], first[0], first[1]], axis=1)
    right = jnp.concatenate([second[0], second[1], second[0]], axis=0)
    return jnp.dot(left, right, preferred_element_type=jnp.float32)


def complex_pair(re, im):
    return jnp.concatenate(
        [jnp.concatenate([re, -im], axis=1), jnp.concatenate([im, re], axis=1)], axis=0
    )


def kernel(
    sizes,
    mode_in, weight_in, energy_in, guess_in, green_in, coupling_in, onsite_in, hopping_in,
    out_ref,
    mode_ref, weight_ref, energy_ref, guess_ref, green_ref, coupling_ref, onsite_ref, hopping_ref,
    halo, own, arrived, total, inverse, before, outer,
    coup_hi, coup_lo, coupt_hi, coupt_lo,
    small_sem, coupling_sem, green_sem, halo_send, halo_recv, kz_send, kz_recv, sp_send, sp_recv,
):
    kz_count, en_count, sp_count = sizes
    energy_count, _, n, _ = green_ref.shape
    ring = kz_count > 2 * REACH
    rows = n // ROW_BLOCKS
    share = n // SHARES
    pieces = 2 * ROW_BLOCKS
    k, en, sp = lax.axis_index("kz"), lax.axis_index("en"), lax.axis_index("sp")
    odd = lax.rem(k, 2)
    sibling = k + 1 - 2 * odd
    back = lax.rem(k + kz_count - REACH, kz_count)
    ahead = lax.rem(k + REACH, kz_count)

    def green_load(e, p):
        return pltpu.make_async_copy(green_in.at[e, p], green_ref.at[e, p], green_sem.at[e, p])

    for p in range(2):
        for e in range(energy_count):
            green_load(e, p).start()
    small_loads = [
        pltpu.make_async_copy(source, target, small_sem.at[index])
        for index, (source, target) in enumerate((
            (mode_in, mode_ref), (weight_in, weight_ref), (energy_in, energy_ref),
            (guess_in, guess_ref), (onsite_in, onsite_ref), (hopping_in, hopping_ref),
        ))
    ]
    coupling_load = pltpu.make_async_copy(coupling_in, coupling_ref, coupling_sem)
    for load in small_loads + [coupling_load]:
        load.start()

    barrier = pltpu.get_barrier_semaphore()

    def greet(axis, index):
        pl.semaphore_signal(barrier, inc=1, device_id={axis: index}, device_id_type=MESH)

    greet("kz", sibling)
    greet("kz", back)
    if ring:
        greet("kz", ahead)
    for axis, here, count in (("en", en, en_count), ("sp", sp, sp_count)):
        pl.when(here > 0)(lambda axis=axis, here=here: greet(axis, here - 1))
        pl.when(here < count - 1)(lambda axis=axis, here=here: greet(axis, here + 1))
    expected = 2 + int(ring)
    for here, count in ((en, en_count), (sp, sp_count)):
        expected = expected + (here > 0).astype(jnp.int32) + (here < count - 1).astype(jnp.int32)
    pl.semaphore_wait(barrier, expected)

    def remote(source, target, send, recv, axis, index):
        return pltpu.make_async_remote_copy(
            src_ref=source, dst_ref=target, send_sem=send, recv_sem=recv,
            device_id={axis: index}, device_id_type=MESH,
        )

    def halo_up(p):
        return remote(green_in.at[energy_count - 1, p], halo.at[0, p],
                      halo_send.at[0, p], halo_recv.at[0, p], "en", en + 1)

    def halo_down(p):
        return remote(green_in.at[0, p], halo.at[1, p],
                      halo_send.at[1, p], halo_recv.at[1, p], "en", en - 1)

    for p in range(2):
        pl.when(en < en_count - 1)(lambda p=p: halo_up(p).start())
        pl.when(en > 0)(lambda p=p: halo_down(p).start())

    @pl.when(en == 0)
    def _():
        halo[0] = jnp.zeros_like(halo[0])

    @pl.when(en == en_count - 1)
    def _():
        halo[1] = jnp.zeros_like(halo[1])

    def energy_of(i):
        return lax.rem(i + en, energy_count)

    def kz_copy(slot, i, p, h, source, index):
        at = pl.ds(h * share, share)
        return remote(source.at[i, p, at], arrived.at[slot, i, p, at], kz_send.at[slot, i, p, h],
                      kz_recv.at[slot, i, p, h], "kz", index)

    def to_back(i, p, h):
        return kz_copy(AHEAD if ring else BACK, i, p, h, own, back)

    def to_ahead(i, p, h):
        return kz_copy(BACK, i, p, h, own, ahead)

    def to_sibling(i, p, h):
        return kz_copy(SIBLING, i, p, h, own, sibling)

    def passing(i, p, h):
        slot = jnp.where(odd == 1, BACK, AHEAD) if ring else BACK
        return kz_copy(PASSED, i, p, h, arrived.at[slot], sibling)

    def issue(i, p):
        e = energy_of(i)
        if i == 0:
            for other in range(energy_count):
                green_load(other, p).wait()

        @pl.when(e > 0)
        def _():
            own[i, p] = green_ref[jnp.maximum(e - 1, 0), p]

        @pl.when(e == 0)
        def _():
            pl.when(en > 0)(lambda: halo_up(p).wait_recv())
            own[i, p] = halo[0, p]

        @pl.when(e < energy_count - 1)
        def _():
            own[i, p] += green_ref[jnp.minimum(e + 1, energy_count - 1), p]

        @pl.when(e == energy_count - 1)
        def _():
            pl.when(en < en_count - 1)(lambda: halo_down(p).wait_recv())
            own[i, p] += halo[1, p]

        for h in range(SHARES):
            to_ahead(i, p, h).start()
            if ring:
                to_back(i, p, h).start()
        for h in range(SHARES):
            to_sibling(i, p, h).start()

    def term(i, p, block, column, first=False):
        mode = mode_ref[column]
        matrix = (coup_hi[mode], coup_lo[mode])
        turned = (coupt_hi[mode], coupt_lo[mode])
        left = dot_split(matrix, split(block)) * weight_ref[mode]
        value = dot_split(split(left), turned)
        if first:
            total[i, p] = value
        else:
            total[i, p] += value

    def own_terms(i, p):
        term(i, p, own[i, p], REACH, first=True)

    def sibling_terms(i, p):
        for h in range(SHARES):
            to_sibling(i, p, h).wait_recv()
        term(i, p, arrived[SIBLING, i, p], 2 * REACH - 1 - 2 * (1 - odd))

    def pass_on(i, p):
        for h in range(SHARES):
            to_ahead(i, p, h).wait_recv()
            if ring:
                to_back(i, p, h).wait_recv()
            passing(i, p, h).start()

    def far_terms(i, p, between):
        term(i, p, arrived[BACK, i, p], 2 * REACH)
        between()
        term(i, p, arrived[AHEAD if ring else BACK, i, p], 0)
        between()

    def passed_terms(i, p):
        for h in range(SHARES):
            passing(i, p, h).wait_recv()
        term(i, p, arrived[PASSED, i, p], 2 * REACH - 1 - 2 * odd)

    def link(i, j):
        p, r = j // ROW_BLOCKS, lax.rem(j, ROW_BLOCKS)
        at = pl.ds(pl.multiple_of(r * rows, rows), rows)
        return remote(out_ref.at[energy_of(i), p, at], before.at[i, p, at],
                      sp_send.at[i, j], sp_recv.at[i, j], "sp", sp + 1)

    def chain_step(i, j):
        p, r = j // ROW_BLOCKS, lax.rem(j, ROW_BLOCKS)
        at = pl.ds(pl.multiple_of(r * rows, rows), rows)
        e = energy_of(i)

        @pl.when(sp > 0)
        def _():
            link(i, j).wait_recv()
            out_ref[e, p, at] = outer[at] * before[i, p, at] + inverse[i, p, at]

        @pl.when(sp == 0)
        def _():
            out_ref[e, p, at] = inverse[i, p, at]

        @pl.when(sp < sp_count - 1)
        def _():
            link(i, j).start()

    def invert(i, between, emit):
        e = energy_of(i)
        guess = guess_ref[e]
        shift = onsite_ref[...] - energy_ref[e]
        diagonal = (lax.broadcasted_iota(jnp.int32, (n, n), 0)
                    == lax.broadcasted_iota(jnp.int32, (n, n), 1))
        r_re = jnp.where(diagonal, 1.0 - guess * shift, 0.0) - guess * total[i, 0]
        r_im = -guess * total[i, 1]

        def stack(re, im):
            return tuple(
                jnp.concatenate([a, b], axis=0) for a, b in zip(split(re), split(im))
            )

        def left(re, im):
            return tuple(complex_pair(a, b) for a, b in zip(split(re), split(im)))

        r_left = left(r_re, r_im)
        square = dot_split(r_left, stack(r_re, r_im))
        between()
        s_re, s_im = square[:n], square[n:]
        s_stack = stack(s_re, s_im)
        cube = dot_split(r_left, s_stack)
        fourth = dot_split(left(s_re, s_im), s_stack)
        between()
        one = jnp.where(diagonal, 1.0, 0.0)
        p_re = one + r_re + s_re + cube[:n]
        p_im = r_im + s_im + cube[n:]
        re, im = split(p_re), split(p_im)
        fourth = stack(fourth[:n], fourth[n:])
        sides = [(a, -b) for a, b in zip(re, im)], list(zip(im, re))
        for p, (side, whole) in enumerate(zip(sides, (p_re, p_im))):
            rows_left = tuple(jnp.concatenate(pair, axis=1) for pair in side)
            inverse[i, p] = guess * (whole + dot_split(rows_left, fourth))
            emit(p)

    for p in range(2):
        issue(0, p)
    for load in small_loads + [coupling_load]:
        load.wait()
    for mode in range(coupling_ref.shape[0]):
        matrix = coupling_ref[mode]
        coup_hi[mode], coup_lo[mode] = split(matrix)
        coupt_hi[mode], coupt_lo[mode] = split(matrix.T)
    across = jnp.broadcast_to(hopping_ref[...], (n, n))
    outer[...] = across * across.T

    pending = []

    def paced(i, t):
        group = t - sp

        @pl.when((sp > 0) & (group >= 0) & (group < pieces // PACE))
        def _():
            for step in range(PACE):
                chain_step(i, group * PACE + step)

    def between():
        if pending:
            i, t = pending[0]
            paced(i, t)
            pending[0] = (i, t + 1)

    def finish():
        if pending:
            i, t = pending.pop()

            @pl.loop(t, pieces // PACE + sp_count - 1)
            def _(t):
                paced(i, t)

    def chain_part(i, p):
        @pl.loop(p * ROW_BLOCKS, (p + 1) * ROW_BLOCKS)
        def _(j):
            chain_step(i, j)

    for p in range(2):
        own_terms(0, p)
        sibling_terms(0, p)
    for i in range(energy_count):
        last = i == energy_count - 1
        for p in range(2):
            if not last:
                issue(i + 1, p)
            if i > 0 and p == 1:
                for _ in range(WAITING):
                    between()
            if i == 0 or p == 1:
                pass_on(i, p)
            if not last:
                own_terms(i + 1, p)
            far_terms(i, p, between)
            if not last:
                sibling_terms(i + 1, p)
            passed_terms(i, p)
            between()
        if not last:
            called = []

            def early(i=i, called=called):
                between()
                if called:
                    pass_on(i + 1, 0)
                called.append(1)

            def emit(p, i=i):
                if p == 0:
                    finish()
                pl.when(sp == 0)(lambda: chain_part(i, p))

            invert(i, early, emit)
            pending.append((i, 1))
        else:

            def emit(p, i=i):
                if p == 0:
                    finish()
                chain_part(i, p)

            invert(i, between, emit)

    for p in range(2):
        pl.when(en < en_count - 1)(lambda p=p: halo_up(p).wait_send())
        pl.when(en > 0)(lambda p=p: halo_down(p).wait_send())
    for i in range(energy_count):
        for p in range(2):
            for h in range(SHARES):
                to_ahead(i, p, h).wait_send()
                if ring:
                    to_back(i, p, h).wait_send()
                to_sibling(i, p, h).wait_send()
                passing(i, p, h).wait_send()

        @pl.when(sp < sp_count - 1)
        def _():
            @pl.loop(0, pieces)
            def _(j):
                link(i, j).wait_send()


def body(sizes, green, coupling, phonon_weight, mode_index, onsite, hopping, energies, guess_scale):
    energy_count, n = green.shape[1], green.shape[-1]
    modes = coupling.shape[1]
    blocks = (energy_count, 2, n, n)
    slots = 4 if sizes[0] > 2 * REACH else 3
    pieces = 2 * ROW_BLOCKS
    hbm = pl.BlockSpec(memory_space=pltpu.HBM)
    vmem = pl.BlockSpec(memory_space=pltpu.VMEM)
    half = pltpu.VMEM((modes, n, n), jnp.bfloat16)
    out = pl.pallas_call(
        functools.partial(kernel, sizes),
        out_shape=jax.ShapeDtypeStruct(blocks, jnp.float32),
        in_specs=[hbm] * 8,
        out_specs=vmem,
        scratch_shapes=[
            pltpu.SMEM(mode_index.shape[1:], jnp.int32),
            pltpu.SMEM(phonon_weight.shape, jnp.float32),
            pltpu.SMEM((energy_count,), jnp.float32),
            pltpu.SMEM((energy_count,), jnp.float32),
            pltpu.VMEM(blocks, jnp.float32),
            pltpu.VMEM(coupling.shape[1:], jnp.float32),
            pltpu.VMEM((1, n), jnp.float32),
            pltpu.VMEM((1, n), jnp.float32),
            pltpu.VMEM((2, 2, n, n), jnp.float32),
            pltpu.VMEM(blocks, jnp.float32),
            pltpu.VMEM((slots,) + blocks, jnp.float32),
            pltpu.VMEM(blocks, jnp.float32),
            pltpu.VMEM(blocks, jnp.float32),
            pltpu.VMEM(blocks, jnp.float32),
            pltpu.VMEM((n, n), jnp.float32),
            half, half, half, half,
            pltpu.SemaphoreType.DMA((6,)),
            pltpu.SemaphoreType.DMA,
            pltpu.SemaphoreType.DMA((energy_count, 2)),
            pltpu.SemaphoreType.DMA((2, 2)),
            pltpu.SemaphoreType.DMA((2, 2)),
            pltpu.SemaphoreType.DMA((slots, energy_count, 2, SHARES)),
            pltpu.SemaphoreType.DMA((slots, energy_count, 2, SHARES)),
            pltpu.SemaphoreType.DMA((energy_count, pieces)),
            pltpu.SemaphoreType.DMA((energy_count, pieces)),
        ],
        compiler_params=pltpu.CompilerParams(
            collective_id=0, has_side_effects=True, vmem_limit_bytes=50 << 20
        ),
    )(
        *(
            pltpu.with_memory_space_constraint(value, pltpu.HBM)
            for value in (
                mode_index[0], phonon_weight, energies, guess_scale.reshape(energy_count),
                green.reshape(blocks), coupling[0], onsite, hopping,
            )
        )
    )
    return out.reshape(1, energy_count, 1, 2, n, n)


def solution(mesh):
    placed = (
        P("kz", "en", "sp", None, None, None),
        P("sp", None, None, None),
        P(),
        P("kz", None),
        P("sp", None),
        P("sp", None),
        P("en"),
        P("kz", "en", "sp"),
    )
    sizes = tuple(mesh.shape[axis] for axis in ("kz", "en", "sp"))
    return jax.shard_map(
        functools.partial(body, sizes),
        mesh=mesh,
        in_specs=placed,
        out_specs=P("kz", "en", "sp", None, None, None),
        check_vma=False,
    )
```

profile of v0, /device:TPU:24, one launch (start us, length us, event | category | flops | bytes accessed | tf_op | source)
XLA Modules:
  0.0 52.5 jit_solution(2198626889769413534)
XLA Ops:
  0.0 51.5 %shard_map.82 = f32[2,2,256,256]{3,2,1,0:T(8,128)S(1)} custom-call(s32[5]{0:T(128)} %bitcast.10, f32[3]{0:T(128)} %weight_in.1, f32[2]{0:T(128)} %energy_in.1, f32[2]{0:T(128)} %bitcast.11, f32[2,2,256,256]{3,2,1,0:T(8,128)} %bitcast.8, f32[3,256,256]{2,1,0:T(8,128)} %bitcast.9, f32[1,256]{1,0:T(1,128)} %onsite_in.1, f32[1,256]{1,0:T(1,128)} %hopping_in.1), custom_call_target="tpu_custom_call" | custom-call | tf_op jit(solution)/shard_map/pallas_call | solution.py:380
  51.5 1.0 %copy.11 = f32[1,2,1,2,256,256]{5,4,3,2,1,0:T(8,128)} copy(f32[1,2,1,2,256,256]{5,4,3,2,1,0:T(8,128)S(1)} %bitcast.7) | data formatting | bytes 2097152
where the time goes:
time: 52.6 us; the launch traced here: 52.5 us
  Pallas kernels  51.5 us (98%)
  local copies, waits for them, and re-layouts  0.97 us (2%)
    pallas_call x1, Pallas kernels, body(): pl.pallas_call(functools.partial(kernel, sizes), out_shape=jax.ShapeDtype...  51.5 us

commit v1 on v0

v1 whole, which is shorter than its diff:
```python
import functools

import jax
import jax.numpy as jnp
from jax import lax
from jax.experimental import pallas as pl
from jax.experimental.pallas import tpu as pltpu
from jax.sharding import PartitionSpec as P

REACH = 2
ROW_BLOCKS = 8
MESH = pl.DeviceIdType.MESH


def split(value):
    high = value.astype(jnp.bfloat16)
    return high, (value - high.astype(jnp.float32)).astype(jnp.bfloat16)


def dot_split(first, second):
    left = jnp.concatenate([first[0], first[0], first[1]], axis=1)
    right = jnp.concatenate([second[0], second[1], second[0]], axis=0)
    return jnp.dot(left, right, preferred_element_type=jnp.float32)


def complex_pair(re, im):
    return jnp.concatenate(
        [jnp.concatenate([re, -im], axis=1), jnp.concatenate([im, re], axis=1)], axis=0
    )


def kernel(
    sizes,
    mode_in, weight_in, energy_in, guess_in, green_in, coupling_in, onsite_in, hopping_in,
    out_ref,
    mode_ref, mode_sib, mode_far, weight_ref, energy_ref, guess_ref,
    green_ref, coupling_ref, onsite_ref, hopping_ref,
    halo, left3, right3, block3, terms, total, sib_out, sib_in, part_out, part_in, message, arrived,
    inverse, before, outer,
    small_sem, coupling_sem, green_sem, mode_send, mode_recv, halo_send, halo_recv,
    sib_send, sib_recv, part_send, part_recv, kz_send, kz_recv, sp_send, sp_recv,
):
    kz_count, en_count, sp_count = sizes
    energy_count, _, n, _ = green_ref.shape
    modes = coupling_ref.shape[0]
    ring = kz_count > 2 * REACH
    steps = (REACH, -REACH) if ring else (REACH,)
    messages = [(d, t) for d in range(len(steps)) for t in range(2)]
    half = n // 2
    rows = n // ROW_BLOCKS
    pieces = 2 * ROW_BLOCKS
    k, en, sp = lax.axis_index("kz"), lax.axis_index("en"), lax.axis_index("sp")
    odd = lax.rem(k, 2)
    base = k - odd
    sibling = base + 1 - odd

    def far(d, t):
        return lax.rem(base + t + steps[d] + kz_count, kz_count)

    def origin(d, t):
        return lax.rem(base + t - steps[d] + kz_count, kz_count)

    def green_load(e, p):
        return pltpu.make_async_copy(green_in.at[e, p], green_ref.at[e, p], green_sem.at[e, p])

    coupling_load = pltpu.make_async_copy(coupling_in, coupling_ref, coupling_sem)
    small_loads = [
        pltpu.make_async_copy(source, target, small_sem.at[index])
        for index, (source, target) in enumerate((
            (mode_in, mode_ref), (weight_in, weight_ref), (energy_in, energy_ref),
            (guess_in, guess_ref), (onsite_in, onsite_ref), (hopping_in, hopping_ref),
        ))
    ]
    coupling_load.start()
    for p in range(2):
        for e in range(energy_count):
            green_load(e, p).start()
    for load in small_loads:
        load.start()

    barrier = pltpu.get_barrier_semaphore()

    def greet(axis, index):
        pl.semaphore_signal(barrier, inc=1, device_id={axis: index}, device_id_type=MESH)

    greet("kz", sibling)
    for d, t in messages:
        greet("kz", far(d, t))
    for axis, here, count in (("en", en, en_count), ("sp", sp, sp_count)):
        pl.when(here > 0)(lambda axis=axis, here=here: greet(axis, here - 1))
        pl.when(here < count - 1)(lambda axis=axis, here=here: greet(axis, here + 1))
    expected = 1 + len(messages)
    for here, count in ((en, en_count), (sp, sp_count)):
        expected = expected + (here > 0).astype(jnp.int32) + (here < count - 1).astype(jnp.int32)
    pl.semaphore_wait(barrier, expected)

    def remote(source, target, send, recv, axis, index):
        return pltpu.make_async_remote_copy(
            src_ref=source, dst_ref=target, send_sem=send, recv_sem=recv,
            device_id={axis: index}, device_id_type=MESH,
        )

    def halo_up(p):
        return remote(green_in.at[energy_count - 1, p], halo.at[0, p],
                      halo_send.at[0, p], halo_recv.at[0, p], "en", en + 1)

    def halo_down(p):
        return remote(green_in.at[0, p], halo.at[1, p],
                      halo_send.at[1, p], halo_recv.at[1, p], "en", en - 1)

    def mode_to_sibling():
        return remote(mode_in, mode_sib, mode_send.at[2 * len(steps) * 2],
                      mode_recv.at[len(messages)], "kz", sibling)

    def mode_to_origin(d, t, slot):
        return remote(mode_in, mode_far.at[2 * d + slot], mode_send.at[2 * d + t],
                      mode_recv.at[2 * d + slot], "kz", origin(d, t))

    mode_to_sibling().start()
    for d, t in messages:
        mode_to_origin(d, t, odd).start()
    for p in range(2):
        pl.when(en < en_count - 1)(lambda p=p: halo_up(p).start())
        pl.when(en > 0)(lambda p=p: halo_down(p).start())

    @pl.when(en == 0)
    def _():
        halo[0] = jnp.zeros_like(halo[0])

    @pl.when(en == en_count - 1)
    def _():
        halo[1] = jnp.zeros_like(halo[1])

    def energy_of(i):
        return lax.rem(i + en, energy_count)

    def load_block(i, p):
        e = energy_of(i)

        def keep(value):
            high, low = split(value)
            block3[0:n] = high
            block3[n:2 * n] = low
            block3[2 * n:] = high

        below = green_ref[jnp.maximum(e - 1, 0), p]
        above = green_ref[jnp.minimum(e + 1, energy_count - 1), p]

        @pl.when((e > 0) & (e < energy_count - 1))
        def _():
            keep(below + above)

        @pl.when(e == 0)
        def _():
            pl.when(en > 0)(lambda: halo_up(p).wait_recv())
            keep(halo[0, p] + above)

        @pl.when((e > 0) & (e == energy_count - 1))
        def _():
            pl.when(en < en_count - 1)(lambda: halo_down(p).wait_recv())
            keep(below + halo[1, p])

    def mode_terms(side):
        first = jnp.dot(left3[side], block3[...], preferred_element_type=jnp.float32)
        for m in range(modes):
            high, low = split(first[m * half:(m + 1) * half])
            terms[m] = jnp.dot(
                jnp.concatenate([high, high, low], axis=1), right3[m],
                preferred_element_type=jnp.float32,
            )

    def contribution(d, t):
        row = mode_far.at[2 * d + t]
        same = odd == t
        near = 2 * REACH - 1 if t == 0 else 1
        if not ring:
            mode = jnp.where(same, row[2 * REACH], row[near])
            other = row[0]
            return terms[mode] + same.astype(jnp.float32) * terms[other]
        end = 2 * REACH if d == 0 else 0
        if t == d:
            return terms[jnp.where(same, row[end], row[near])]
        return same.astype(jnp.float32) * terms[row[end]]

    def to_sibling(i, p):
        return remote(sib_out.at[i, p], sib_in.at[i, p], sib_send.at[i, p],
                      sib_recv.at[i, p], "kz", sibling)

    def part(i, p, j):
        return remote(part_out.at[i, p, j], part_in.at[i, p, j], part_send.at[i, p, j],
                      part_recv.at[i, p, j], "kz", sibling)

    def over(i, p, j, side):
        d, t = messages[j]
        return remote(message.at[i, p, j],
                      arrived.at[d, i, p, pl.ds(pl.multiple_of(side * half, half), half)],
                      kz_send.at[i, p, j], kz_recv.at[d, i, p, side], "kz", far(d, t))

    def half_terms(i, p, own):
        side = odd if own else 1 - odd
        mode_terms(side)
        at = pl.ds(pl.multiple_of(side * half, half), half)
        for j, (d, t) in enumerate(messages):
            if own:
                message[i, p, j] = contribution(d, t)
            else:
                part_out[i, p, j] = contribution(d, t)
                part(i, p, j).start()
        sib_out[i, p, at] = terms[mode_sib[REACH + 1 - 2 * odd]]
        if own:
            to_sibling(i, p).start()
        total[i, p, at] = terms[mode_ref[REACH]]

    def assemble(i, p, j):
        part(i, p, j).wait_recv()
        message[i, p, j] += part_in[i, p, j]
        over(i, p, j, odd).start()

    def gather(i, p):
        to_sibling(i, p).wait_recv()
        total[i, p] += sib_in[i, p]

    def collect(i, p):
        value = total[i, p]
        for d in range(len(steps)):
            for side in range(2):
                over(i, p, 2 * d, side).wait_recv()
            value = value + arrived[d, i, p]
        return value

    def place(j):
        block, rest = j // ROW_BLOCKS, lax.rem(j, ROW_BLOCKS)
        p, r = rest // (ROW_BLOCKS // 2), lax.rem(rest, ROW_BLOCKS // 2)
        return p, pl.ds(pl.multiple_of(block * half + r * rows, rows), rows)

    def link(i, j):
        p, at = place(j)
        return remote(out_ref.at[energy_of(i), p, at], before.at[i, p, at],
                      sp_send.at[i, j], sp_recv.at[i, j], "sp", sp + 1)

    def chain_step(i, j):
        p, at = place(j)
        e = energy_of(i)

        @pl.when(sp > 0)
        def _():
            link(i, j).wait_recv()
            out_ref[e, p, at] = outer[at] * before[i, p, at] + inverse[i, p, at]

        @pl.when(sp == 0)
        def _():
            out_ref[e, p, at] = inverse[i, p, at]

        @pl.when(sp < sp_count - 1)
        def _():
            link(i, j).start()

    def chain_part(i, first, last):
        @pl.loop(first, last)
        def _(j):
            chain_step(i, j)

    def invert(i):
        e = energy_of(i)
        guess = guess_ref[e]
        shift = onsite_ref[...] - energy_ref[e]
        diagonal = (lax.broadcasted_iota(jnp.int32, (n, n), 0)
                    == lax.broadcasted_iota(jnp.int32, (n, n), 1))
        r_re = jnp.where(diagonal, 1.0 - guess * shift, 0.0) - guess * collect(i, 0)
        r_im = -guess * collect(i, 1)

        def stack(re, im):
            return tuple(
                jnp.concatenate([a, b], axis=0) for a, b in zip(split(re), split(im))
            )

        def left(re, im):
            return tuple(complex_pair(a, b) for a, b in zip(split(re), split(im)))

        r_left = left(r_re, r_im)
        square = dot_split(r_left, stack(r_re, r_im))
        s_re, s_im = square[:n], square[n:]
        s_stack = stack(s_re, s_im)
        cube = dot_split(r_left, s_stack)
        fourth = dot_split(left(s_re, s_im), s_stack)
        one = jnp.where(diagonal, 1.0, 0.0)
        p_re = one + r_re + s_re + cube[:n]
        p_im = r_im + s_im + cube[n:]
        re, im = split(p_re), split(p_im)
        fourth = stack(fourth[:n], fourth[n:])
        for block in range(2):
            at = slice(block * half, (block + 1) * half)
            rows_left = tuple(complex_pair(a[at], b[at]) for a, b in zip(re, im))
            result = dot_split(rows_left, fourth)
            inverse[i, 0, at] = guess * (p_re[at] + result[:half])
            inverse[i, 1, at] = guess * (p_im[at] + result[half:])
            pl.when(sp == 0)(lambda: chain_part(i, block * ROW_BLOCKS, (block + 1) * ROW_BLOCKS))

    for load in small_loads:
        load.wait()
    coupling_load.wait()
    for mode in range(modes):
        matrix = coupling_ref[mode]
        high, low = split(matrix)
        for side in range(2):
            at = slice(mode * half, (mode + 1) * half)
            here = slice(side * half, (side + 1) * half)
            left3[side, at] = jnp.concatenate([high[here], high[here], low[here]], axis=1)
        high, low = split(matrix.T * weight_ref[mode])
        right3[mode] = jnp.concatenate([high, low, high], axis=0)
    for p in range(2):
        for e in range(energy_count):
            green_load(e, p).wait()

    evens = [j for j, (d, t) in enumerate(messages) if t == 0]
    odds = [j for j, (d, t) in enumerate(messages) if t == 1]

    def wait_modes():
        mode_to_sibling().wait_recv()
        for d, t in messages:
            mode_to_origin(d, t, t).wait_recv()

    load_block(0, 0)
    wait_modes()
    half_terms(0, 0, False)
    half_terms(0, 0, True)
    load_block(0, 1)
    half_terms(0, 1, False)
    for j in evens:
        assemble(0, 0, j)
    half_terms(0, 1, True)
    for j in evens:
        assemble(0, 1, j)
    for j in odds:
        for p in range(2):
            assemble(0, p, j)
    across = jnp.broadcast_to(hopping_ref[...], (n, n))
    outer[...] = across * across.T
    for i in range(energy_count):
        last = i == energy_count - 1

        def second(i=i):
            load_block(i + 1, 1)
            half_terms(i + 1, 1, False)
            half_terms(i + 1, 1, True)
            for j in evens:
                assemble(i + 1, 1, j)
            for j in odds:
                for p in range(2):
                    assemble(i + 1, p, j)

        for p in range(2):
            gather(i, p)
        if not last:
            load_block(i + 1, 0)
            half_terms(i + 1, 0, False)
            half_terms(i + 1, 0, True)
            for j in evens:
                assemble(i + 1, 0, j)
            pl.when(odd == 1)(second)
        invert(i)
        if not last:
            pl.when(odd == 0)(second)
        pl.when(sp > 0)(lambda i=i: chain_part(i, 0, pieces))

    mode_to_sibling().wait_send()
    for d, t in messages:
        mode_to_origin(d, t, odd).wait_send()
    for p in range(2):
        pl.when(en < en_count - 1)(lambda p=p: halo_up(p).wait_send())
        pl.when(en > 0)(lambda p=p: halo_down(p).wait_send())
    for i in range(energy_count):
        for p in range(2):
            to_sibling(i, p).wait_send()
            for j in range(len(messages)):
                part(i, p, j).wait_send()
                over(i, p, j, odd).wait_send()

        @pl.when(sp < sp_count - 1)
        def _():
            @pl.loop(0, pieces)
            def _(j):
                link(i, j).wait_send()


def body(sizes, green, coupling, phonon_weight, mode_index, onsite, hopping, energies, guess_scale):
    energy_count, n = green.shape[1], green.shape[-1]
    modes = coupling.shape[1]
    blocks = (energy_count, 2, n, n)
    steps = 2 if sizes[0] > 2 * REACH else 1
    halves = (energy_count, 2, 2 * steps, n // 2, n)
    pieces = 2 * ROW_BLOCKS
    hbm = pl.BlockSpec(memory_space=pltpu.HBM)
    vmem = pl.BlockSpec(memory_space=pltpu.VMEM)
    columns = mode_index.shape[1]
    dma = pltpu.SemaphoreType.DMA
    out = pl.pallas_call(
        functools.partial(kernel, sizes),
        out_shape=jax.ShapeDtypeStruct(blocks, jnp.float32),
        in_specs=[hbm] * 8,
        out_specs=vmem,
        scratch_shapes=[
            pltpu.SMEM((columns,), jnp.int32),
            pltpu.SMEM((columns,), jnp.int32),
            pltpu.SMEM((2 * steps, columns), jnp.int32),
            pltpu.SMEM(phonon_weight.shape, jnp.float32),
            pltpu.SMEM((energy_count,), jnp.float32),
            pltpu.SMEM((energy_count,), jnp.float32),
            pltpu.VMEM(blocks, jnp.float32),
            pltpu.VMEM(coupling.shape[1:], jnp.float32),
            pltpu.VMEM((1, n), jnp.float32),
            pltpu.VMEM((1, n), jnp.float32),
            pltpu.VMEM((2, 2, n, n), jnp.float32),
            pltpu.VMEM((2, modes * n // 2, 3 * n), jnp.bfloat16),
            pltpu.VMEM((modes, 3 * n, n), jnp.bfloat16),
            pltpu.VMEM((3 * n, n), jnp.bfloat16),
            pltpu.VMEM((modes, n // 2, n), jnp.float32),
            pltpu.VMEM(blocks, jnp.float32),
            pltpu.VMEM(blocks, jnp.float32),
            pltpu.VMEM(blocks, jnp.float32),
            pltpu.VMEM(halves, jnp.float32),
            pltpu.VMEM(halves, jnp.float32),
            pltpu.VMEM(halves, jnp.float32),
            pltpu.VMEM((steps,) + blocks, jnp.float32),
            pltpu.VMEM(blocks, jnp.float32),
            pltpu.VMEM(blocks, jnp.float32),
            pltpu.VMEM((n, n), jnp.float32),
            dma((6,)),
            dma,
            dma((energy_count, 2)),
            dma((4 * steps + 1,)),
            dma((2 * steps + 1,)),
            dma((2, 2)),
            dma((2, 2)),
            dma((energy_count, 2)),
            dma((energy_count, 2)),
            dma((energy_count, 2, 2 * steps)),
            dma((energy_count, 2, 2 * steps)),
            dma((energy_count, 2, 2 * steps)),
            dma((steps, energy_count, 2, 2)),
            dma((energy_count, pieces)),
            dma((energy_count, pieces)),
        ],
        compiler_params=pltpu.CompilerParams(
            collective_id=0, has_side_effects=True, vmem_limit_bytes=50 << 20
        ),
    )(
        *(
            pltpu.with_memory_space_constraint(value, pltpu.HBM)
            for value in (
                mode_index[0], phonon_weight, energies, guess_scale.reshape(energy_count),
                green.reshape(blocks), coupling[0], onsite, hopping,
            )
        )
    )
    return out.reshape(1, energy_count, 1, 2, n, n)


def solution(mesh):
    placed = (
        P("kz", "en", "sp", None, None, None),
        P("sp", None, None, None),
        P(),
        P("kz", None),
        P("sp", None),
        P("sp", None),
        P("en"),
        P("kz", "en", "sp"),
    )
    sizes = tuple(mesh.shape[axis] for axis in ("kz", "en", "sp"))
    return jax.shard_map(
        functools.partial(body, sizes),
        mesh=mesh,
        in_specs=placed,
        out_specs=P("kz", "en", "sp", None, None, None),
        check_vma=False,
    )
```

time: 52.6 us -> 49.2 us (0.935)
  the two profiles are of different devices: /device:TPU:24 before, /device:TPU:29 now
where the time goes in v1:
time: 49.2 us; the launch traced here: 49 us
  Pallas kernels  48 us (98%)
  local copies, waits for them, and re-layouts  0.97 us (2%)
    pallas_call x1, Pallas kernels, body(): pl.pallas_call(functools.partial(kernel, sizes), out_shape=jax.ShapeDtype...  48 us

profile of v1, /device:TPU:29, one launch (start us, length us, event | category | flops | bytes accessed | tf_op | source)
XLA Modules:
  0.0 49.0 jit_solution(7476676778072711699)
XLA Ops:
  0.0 48.0 %shard_map.82 = f32[2,2,256,256]{3,2,1,0:T(8,128)S(1)} custom-call(s32[5]{0:T(128)} %bitcast.10, f32[3]{0:T(128)} %weight_in.1, f32[2]{0:T(128)} %energy_in.1, f32[2]{0:T(128)} %bitcast.11, f32[2,2,256,256]{3,2,1,0:T(8,128)} %bitcast.8, f32[3,256,256]{2,1,0:T(8,128)} %bitcast.9, f32[1,256]{1,0:T(1,128)} %onsite_in.1, f32[1,256]{1,0:T(1,128)} %hopping_in.1), custom_call_target="tpu_custom_call" | custom-call | tf_op jit(solution)/shard_map/pallas_call | solution.py:397
  48.0 1.0 %copy.11 = f32[1,2,1,2,256,256]{5,4,3,2,1,0:T(8,128)} copy(f32[1,2,1,2,256,256]{5,4,3,2,1,0:T(8,128)S(1)} %bitcast.7) | data formatting | bytes 2097152

commit v2 on v1

--- a/solution.py
+++ b/solution.py
@@ -33,12 +33,11 @@
     sizes,
     mode_in, weight_in, energy_in, guess_in, green_in, coupling_in, onsite_in, hopping_in,
     out_ref,
-    mode_ref, mode_sib, mode_far, weight_ref, energy_ref, guess_ref,
+    mode_near, mode_far, weight_ref, energy_ref, guess_ref,
     green_ref, coupling_ref, onsite_ref, hopping_ref,
-    halo, left3, right3, block3, terms, total, sib_out, sib_in, part_out, part_in, message, arrived,
-    inverse, before, outer,
+    halo, left3, right3, terms, blocks, near, message, arrived, inverse, before, outer,
     small_sem, coupling_sem, green_sem, mode_send, mode_recv, halo_send, halo_recv,
-    sib_send, sib_recv, part_send, part_recv, kz_send, kz_recv, sp_send, sp_recv,
+    block_send, block_recv, near_send, near_recv, kz_send, kz_recv, sp_send, sp_recv,
 ):
     kz_count, en_count, sp_count = sizes
     energy_count, _, n, _ = green_ref.shape
@@ -67,14 +66,15 @@
     small_loads = [
         pltpu.make_async_copy(source, target, small_sem.at[index])
         for index, (source, target) in enumerate((
-            (mode_in, mode_ref), (weight_in, weight_ref), (energy_in, energy_ref),
+            (mode_in, mode_near.at[odd]), (weight_in, weight_ref), (energy_in, energy_ref),
             (guess_in, guess_ref), (onsite_in, onsite_ref), (hopping_in, hopping_ref),
         ))
     ]
-    coupling_load.start()
     for p in range(2):
         for e in range(energy_count):
             green_load(e, p).start()
+        if p == 0:
+            coupling_load.start()
     for load in small_loads:
         load.start()
 
@@ -108,15 +108,15 @@
         return remote(green_in.at[0, p], halo.at[1, p],
                       halo_send.at[1, p], halo_recv.at[1, p], "en", en - 1)
 
-    def mode_to_sibling():
-        return remote(mode_in, mode_sib, mode_send.at[2 * len(steps) * 2],
+    def mode_to_sibling(parity):
+        return remote(mode_in, mode_near.at[parity], mode_send.at[2 * len(steps)],
                       mode_recv.at[len(messages)], "kz", sibling)
 
     def mode_to_origin(d, t, slot):
         return remote(mode_in, mode_far.at[2 * d + slot], mode_send.at[2 * d + t],
                       mode_recv.at[2 * d + slot], "kz", origin(d, t))
 
-    mode_to_sibling().start()
+    mode_to_sibling(odd).start()
     for d, t in messages:
         mode_to_origin(d, t, odd).start()
     for p in range(2):
@@ -134,61 +134,42 @@
     def energy_of(i):
         return lax.rem(i + en, energy_count)
 
+    def swap(i, p, parity):
+        return remote(blocks.at[parity, i, p], blocks.at[parity, i, p], block_send.at[i, p],
+                      block_recv.at[i, p], "kz", sibling)
+
     def load_block(i, p):
         e = energy_of(i)
-
-        def keep(value):
-            high, low = split(value)
-            block3[0:n] = high
-            block3[n:2 * n] = low
-            block3[2 * n:] = high
-
         below = green_ref[jnp.maximum(e - 1, 0), p]
         above = green_ref[jnp.minimum(e + 1, energy_count - 1), p]
 
         @pl.when((e > 0) & (e < energy_count - 1))
         def _():
-            keep(below + above)
+            blocks[odd, i, p] = below + above
 
         @pl.when(e == 0)
         def _():
             pl.when(en > 0)(lambda: halo_up(p).wait_recv())
-            keep(halo[0, p] + above)
+            blocks[odd, i, p] = halo[0, p] + above
 
         @pl.when((e > 0) & (e == energy_count - 1))
         def _():
             pl.when(en < en_count - 1)(lambda: halo_down(p).wait_recv())
-            keep(below + halo[1, p])
-
-    def mode_terms(side):
-        first = jnp.dot(left3[side], block3[...], preferred_element_type=jnp.float32)
-        for m in range(modes):
-            high, low = split(first[m * half:(m + 1) * half])
-            terms[m] = jnp.dot(
-                jnp.concatenate([high, high, low], axis=1), right3[m],
-                preferred_element_type=jnp.float32,
-            )
-
-    def contribution(d, t):
-        row = mode_far.at[2 * d + t]
-        same = odd == t
-        near = 2 * REACH - 1 if t == 0 else 1
-        if not ring:
-            mode = jnp.where(same, row[2 * REACH], row[near])
-            other = row[0]
-            return terms[mode] + same.astype(jnp.float32) * terms[other]
-        end = 2 * REACH if d == 0 else 0
-        if t == d:
-            return terms[jnp.where(same, row[end], row[near])]
-        return same.astype(jnp.float32) * terms[row[end]]
-
-    def to_sibling(i, p):
-        return remote(sib_out.at[i, p], sib_in.at[i, p], sib_send.at[i, p],
-                      sib_recv.at[i, p], "kz", sibling)
-
-    def part(i, p, j):
-        return remote(part_out.at[i, p, j], part_in.at[i, p, j], part_send.at[i, p, j],
-                      part_recv.at[i, p, j], "kz", sibling)
+            blocks[odd, i, p] = below + halo[1, p]
+
+        swap(i, p, odd).start()
+
+    def columns(d, t, source):
+        if source == t:
+            if not ring:
+                return (2 * REACH, 0)
+            return (2 * REACH,) if d == 0 else (0,)
+        if not ring or t == d:
+            return (2 * REACH - 1,) if t == 0 else (1,)
+        return ()
+
+    def picked(row, column, source):
+        return terms[row[column], pl.ds(source * half, half)]
 
     def over(i, p, j, side):
         d, t = messages[j]
@@ -196,32 +177,49 @@
                       arrived.at[d, i, p, pl.ds(pl.multiple_of(side * half, half), half)],
                       kz_send.at[i, p, j], kz_recv.at[d, i, p, side], "kz", far(d, t))
 
-    def half_terms(i, p, own):
-        side = odd if own else 1 - odd
-        mode_terms(side)
-        at = pl.ds(pl.multiple_of(side * half, half), half)
+    def near_half(i, p, parity, side):
+        at = near.at[parity, i, p, pl.ds(pl.multiple_of(side * half, half), half)]
+        return remote(at, at, near_send.at[i, p], near_recv.at[i, p], "kz", sibling)
+
+    def block_terms(i, p):
+        swap(i, p, 1 - odd).wait_recv()
+        first = [
+            dot_split((left3[:, :n], left3[:, 2 * n:]), split(blocks[source, i, p]))
+            for source in range(2)
+        ]
+        for m in range(modes):
+            at = slice(m * half, (m + 1) * half)
+            high, low = split(jnp.concatenate([first[0][at], first[1][at]], axis=0))
+            terms[m] = jnp.dot(
+                jnp.concatenate([high, high, low], axis=1), right3[m],
+                preferred_element_type=jnp.float32,
+            )
+
+    def block_messages(i, p):
         for j, (d, t) in enumerate(messages):
-            if own:
-                message[i, p, j] = contribution(d, t)
-            else:
-                part_out[i, p, j] = contribution(d, t)
-                part(i, p, j).start()
-        sib_out[i, p, at] = terms[mode_sib[REACH + 1 - 2 * odd]]
-        if own:
-            to_sibling(i, p).start()
-        total[i, p, at] = terms[mode_ref[REACH]]
-
-    def assemble(i, p, j):
-        part(i, p, j).wait_recv()
-        message[i, p, j] += part_in[i, p, j]
-        over(i, p, j, odd).start()
-
-    def gather(i, p):
-        to_sibling(i, p).wait_recv()
-        total[i, p] += sib_in[i, p]
+            message[i, p, j] = sum(
+                picked(mode_far.at[2 * d + t], column, source)
+                for source in range(2) for column in columns(d, t, source)
+            )
+            if t == 0:
+                over(i, p, j, odd).start()
+        at = pl.ds(pl.multiple_of(odd * half, half), half)
+        for t in range(2):
+            near[t, i, p, at] = (
+                picked(mode_near.at[t], REACH, t)
+                + picked(mode_near.at[t], REACH + 2 * t - 1, 1 - t)
+            )
+        near_half(i, p, 1 - odd, odd).start()
+
+    def send_odds(i):
+        for p in range(2):
+            for j, (d, t) in enumerate(messages):
+                if t == 1:
+                    over(i, p, j, odd).start()
 
     def collect(i, p):
-        value = total[i, p]
+        near_half(i, p, odd, 1 - odd).wait_recv()
+        value = near[odd, i, p]
         for d in range(len(steps)):
             for side in range(2):
                 over(i, p, 2 * d, side).wait_recv()
@@ -296,44 +294,30 @@
             inverse[i, 1, at] = guess * (p_im[at] + result[half:])
             pl.when(sp == 0)(lambda: chain_part(i, block * ROW_BLOCKS, (block + 1) * ROW_BLOCKS))
 
+    for e in range(energy_count):
+        green_load(e, 0).wait()
+    load_block(0, 0)
+    for e in range(energy_count):
+        green_load(e, 1).wait()
+    load_block(0, 1)
     for load in small_loads:
         load.wait()
     coupling_load.wait()
-    for mode in range(modes):
-        matrix = coupling_ref[mode]
-        high, low = split(matrix)
-        for side in range(2):
-            at = slice(mode * half, (mode + 1) * half)
-            here = slice(side * half, (side + 1) * half)
-            left3[side, at] = jnp.concatenate([high[here], high[here], low[here]], axis=1)
-        high, low = split(matrix.T * weight_ref[mode])
-        right3[mode] = jnp.concatenate([high, low, high], axis=0)
-    for p in range(2):
-        for e in range(energy_count):
-            green_load(e, p).wait()
-
-    evens = [j for j, (d, t) in enumerate(messages) if t == 0]
-    odds = [j for j, (d, t) in enumerate(messages) if t == 1]
-
-    def wait_modes():
-        mode_to_sibling().wait_recv()
-        for d, t in messages:
-            mode_to_origin(d, t, t).wait_recv()
-
-    load_block(0, 0)
-    wait_modes()
-    half_terms(0, 0, False)
-    half_terms(0, 0, True)
-    load_block(0, 1)
-    half_terms(0, 1, False)
-    for j in evens:
-        assemble(0, 0, j)
-    half_terms(0, 1, True)
-    for j in evens:
-        assemble(0, 1, j)
-    for j in odds:
-        for p in range(2):
-            assemble(0, p, j)
+    for m in range(modes):
+        at = slice(m * half, (m + 1) * half)
+        here = pl.ds(pl.multiple_of(odd * half, half), half)
+        high, low = split(coupling_ref[m, here])
+        left3[at] = jnp.concatenate([high, high, low], axis=1)
+        high, low = split(coupling_ref[m].T * weight_ref[m])
+        right3[m] = jnp.concatenate([high, low, high], axis=0)
+    block_terms(0, 0)
+    mode_to_sibling(1 - odd).wait_recv()
+    for d, t in messages:
+        mode_to_origin(d, t, t).wait_recv()
+    block_messages(0, 0)
+    block_terms(0, 1)
+    block_messages(0, 1)
+    send_odds(0)
     across = jnp.broadcast_to(hopping_ref[...], (n, n))
     outer[...] = across * across.T
     for i in range(energy_count):
@@ -341,29 +325,21 @@
 
         def second(i=i):
             load_block(i + 1, 1)
-            half_terms(i + 1, 1, False)
-            half_terms(i + 1, 1, True)
-            for j in evens:
-                assemble(i + 1, 1, j)
-            for j in odds:
-                for p in range(2):
-                    assemble(i + 1, p, j)
-
-        for p in range(2):
-            gather(i, p)
+            block_terms(i + 1, 1)
+            block_messages(i + 1, 1)
+            send_odds(i + 1)
+
         if not last:
             load_block(i + 1, 0)
-            half_terms(i + 1, 0, False)
-            half_terms(i + 1, 0, True)
-            for j in evens:
-                assemble(i + 1, 0, j)
+            block_terms(i + 1, 0)
+            block_messages(i + 1, 0)
             pl.when(odd == 1)(second)
         invert(i)
         if not last:
             pl.when(odd == 0)(second)
         pl.when(sp > 0)(lambda i=i: chain_part(i, 0, pieces))
 
-    mode_to_sibling().wait_send()
+    mode_to_sibling(odd).wait_send()
     for d, t in messages:
         mode_to_origin(d, t, odd).wait_send()
     for p in range(2):
@@ -371,9 +347,9 @@
         pl.when(en > 0)(lambda p=p: halo_down(p).wait_send())
     for i in range(energy_count):
         for p in range(2):
-            to_sibling(i, p).wait_send()
+            swap(i, p, odd).wait_send()
+            near_half(i, p, 1 - odd, odd).wait_send()
             for j in range(len(messages)):
-                part(i, p, j).wait_send()
                 over(i, p, j, odd).wait_send()
 
         @pl.when(sp < sp_count - 1)
@@ -400,8 +376,7 @@
         in_specs=[hbm] * 8,
         out_specs=vmem,
         scratch_shapes=[
-            pltpu.SMEM((columns,), jnp.int32),
-            pltpu.SMEM((columns,), jnp.int32),
+            pltpu.SMEM((2, columns), jnp.int32),
             pltpu.SMEM((2 * steps, columns), jnp.int32),
             pltpu.SMEM(phonon_weight.shape, jnp.float32),
             pltpu.SMEM((energy_count,), jnp.float32),
@@ -411,15 +386,11 @@
             pltpu.VMEM((1, n), jnp.float32),
             pltpu.VMEM((1, n), jnp.float32),
             pltpu.VMEM((2, 2, n, n), jnp.float32),
-            pltpu.VMEM((2, modes * n // 2, 3 * n), jnp.bfloat16),
+            pltpu.VMEM((modes * n // 2, 3 * n), jnp.bfloat16),
             pltpu.VMEM((modes, 3 * n, n), jnp.bfloat16),
-            pltpu.VMEM((3 * n, n), jnp.bfloat16),
-            pltpu.VMEM((modes, n // 2, n), jnp.float32),
-            pltpu.VMEM(blocks, jnp.float32),
-            pltpu.VMEM(blocks, jnp.float32),
-            pltpu.VMEM(blocks, jnp.float32),
-            pltpu.VMEM(halves, jnp.float32),
-            pltpu.VMEM(halves, jnp.float32),
+            pltpu.VMEM((modes, n, n), jnp.float32),
+            pltpu.VMEM((2,) + blocks, jnp.float32),
+            pltpu.VMEM((2,) + blocks, jnp.float32),
             pltpu.VMEM(halves, jnp.float32),
             pltpu.VMEM((steps,) + blocks, jnp.float32),
             pltpu.VMEM(blocks, jnp.float32),
@@ -428,14 +399,14 @@
             dma((6,)),
             dma,
             dma((energy_count, 2)),
-            dma((4 * steps + 1,)),
+            dma((2 * steps + 1,)),
             dma((2 * steps + 1,)),
             dma((2, 2)),
             dma((2, 2)),
             dma((energy_count, 2)),
             dma((energy_count, 2)),
-            dma((energy_count, 2, 2 * steps)),
-            dma((energy_count, 2, 2 * steps)),
+            dma((energy_count, 2)),
+            dma((energy_count, 2)),
             dma((energy_count, 2, 2 * steps)),
             dma((steps, energy_count, 2, 2)),
             dma((energy_count, pieces)),

time: 49.2 us -> 46.4 us (0.943)
  Pallas kernels: 48 us -> 45.3 us
    pallas_call x1, Pallas kernels: 48 us -> 45.3 us  [body(): pl.pallas_call(functools.partial(kernel, sizes), out_shape=jax.ShapeDtype...]
where the time goes in v2:
time: 46.4 us; the launch traced here: 46.3 us
  Pallas kernels  45.3 us (98%)
  local copies, waits for them, and re-layouts  0.97 us (2%)
    pallas_call x1, Pallas kernels, body(): pl.pallas_call(functools.partial(kernel, sizes), out_shape=jax.ShapeDtype...  45.3 us
    unnamed x1, local copies, waits for them, and re-layouts  0.97 us

profile of v2, /device:TPU:29, one launch (start us, length us, event | category | flops | bytes accessed | tf_op | source)
XLA Modules:
  0.0 46.3 jit_solution(9440402138550623471)
XLA Ops:
  0.0 45.3 %shard_map.82 = f32[2,2,256,256]{3,2,1,0:T(8,128)S(1)} custom-call(s32[5]{0:T(128)} %bitcast.10, f32[3]{0:T(128)} %weight_in.1, f32[2]{0:T(128)} %energy_in.1, f32[2]{0:T(128)} %bitcast.11, f32[2,2,256,256]{3,2,1,0:T(8,128)} %bitcast.8, f32[3,256,256]{2,1,0:T(8,128)} %bitcast.9, f32[1,256]{1,0:T(1,128)} %onsite_in.1, f32[1,256]{1,0:T(1,128)} %hopping_in.1), custom_call_target="tpu_custom_call" | custom-call | tf_op jit(solution)/shard_map/pallas_call | solution.py:373
  45.3 1.0 %copy.11 = f32[1,2,1,2,256,256]{5,4,3,2,1,0:T(8,128)} copy(f32[1,2,1,2,256,256]{5,4,3,2,1,0:T(8,128)S(1)} %bitcast.7) | data formatting | bytes 2097152

commit v3 on v2

--- a/solution.py
+++ b/solution.py
@@ -9,6 +9,7 @@
 
 REACH = 2
 ROW_BLOCKS = 8
+TAKEN = (1, 1, 2, 0, 1, 0)
 MESH = pl.DeviceIdType.MESH
 
 
@@ -36,7 +37,7 @@
     mode_near, mode_far, weight_ref, energy_ref, guess_ref,
     green_ref, coupling_ref, onsite_ref, hopping_ref,
     halo, left3, right3, terms, blocks, near, message, arrived, inverse, before, outer,
-    small_sem, coupling_sem, green_sem, mode_send, mode_recv, halo_send, halo_recv,
+    ready, small_sem, coupling_sem, green_sem, first_sem, mode_send, mode_recv, halo_send, halo_recv,
     block_send, block_recv, near_send, near_recv, kz_send, kz_recv, sp_send, sp_recv,
 ):
     kz_count, en_count, sp_count = sizes
@@ -59,9 +60,13 @@
     def origin(d, t):
         return lax.rem(base + t - steps[d] + kz_count, kz_count)
 
-    def green_load(e, p):
-        return pltpu.make_async_copy(green_in.at[e, p], green_ref.at[e, p], green_sem.at[e, p])
-
+    direct = en_count == 2 and energy_count == 2
+
+    def first_load(p):
+        return pltpu.make_async_copy(green_in.at[1 - en, p], blocks.at[odd, 0, p],
+                                     first_sem.at[p])
+
+    green_load = pltpu.make_async_copy(green_in, green_ref, green_sem)
     coupling_load = pltpu.make_async_copy(coupling_in, coupling_ref, coupling_sem)
     small_loads = [
         pltpu.make_async_copy(source, target, small_sem.at[index])
@@ -70,14 +75,6 @@
             (guess_in, guess_ref), (onsite_in, onsite_ref), (hopping_in, hopping_ref),
         ))
     ]
-    for p in range(2):
-        for e in range(energy_count):
-            green_load(e, p).start()
-        if p == 0:
-            coupling_load.start()
-    for load in small_loads:
-        load.start()
-
     barrier = pltpu.get_barrier_semaphore()
 
     def greet(axis, index):
@@ -87,12 +84,23 @@
     for d, t in messages:
         greet("kz", far(d, t))
     for axis, here, count in (("en", en, en_count), ("sp", sp, sp_count)):
-        pl.when(here > 0)(lambda axis=axis, here=here: greet(axis, here - 1))
         pl.when(here < count - 1)(lambda axis=axis, here=here: greet(axis, here + 1))
+    coupling_load.start()
+    if direct:
+        for p in range(2):
+            first_load(p).start()
+    for load in small_loads:
+        load.start()
+    green_load.start()
     expected = 1 + len(messages)
-    for here, count in ((en, en_count), (sp, sp_count)):
-        expected = expected + (here > 0).astype(jnp.int32) + (here < count - 1).astype(jnp.int32)
+    for here in (en, sp):
+        expected = expected + (here > 0).astype(jnp.int32)
     pl.semaphore_wait(barrier, expected)
+    for index, (axis, here) in enumerate((("en", en), ("sp", sp))):
+        @pl.when(here > 0)
+        def _():
+            pl.semaphore_signal(ready.at[index], inc=1, device_id={axis: here - 1},
+                                device_id_type=MESH)
 
     def remote(source, target, send, recv, axis, index):
         return pltpu.make_async_remote_copy(
@@ -102,11 +110,11 @@
 
     def halo_up(p):
         return remote(green_in.at[energy_count - 1, p], halo.at[0, p],
-                      halo_send.at[0, p], halo_recv.at[0, p], "en", en + 1)
+                      halo_send.at[0], halo_recv.at[0, p], "en", en + 1)
 
     def halo_down(p):
         return remote(green_in.at[0, p], halo.at[1, p],
-                      halo_send.at[1, p], halo_recv.at[1, p], "en", en - 1)
+                      halo_send.at[1], halo_recv.at[1, p], "en", en - 1)
 
     def mode_to_sibling(parity):
         return remote(mode_in, mode_near.at[parity], mode_send.at[2 * len(steps)],
@@ -116,27 +124,30 @@
         return remote(mode_in, mode_far.at[2 * d + slot], mode_send.at[2 * d + t],
                       mode_recv.at[2 * d + slot], "kz", origin(d, t))
 
+    def swap(i, p, parity):
+        source = green_in.at[1 - en, p] if direct and i == 0 else blocks.at[parity, i, p]
+        return remote(source, blocks.at[parity, i, p], block_send, block_recv.at[i, p],
+                      "kz", sibling)
+
     mode_to_sibling(odd).start()
     for d, t in messages:
         mode_to_origin(d, t, odd).start()
+    if direct:
+        for p in range(2):
+            swap(0, p, odd).start()
     for p in range(2):
-        pl.when(en < en_count - 1)(lambda p=p: halo_up(p).start())
         pl.when(en > 0)(lambda p=p: halo_down(p).start())
 
-    @pl.when(en == 0)
-    def _():
-        halo[0] = jnp.zeros_like(halo[0])
-
-    @pl.when(en == en_count - 1)
-    def _():
-        halo[1] = jnp.zeros_like(halo[1])
+    def start_up():
+        @pl.when(en < en_count - 1)
+        def _():
+            pl.semaphore_wait(ready.at[0], 1)
+            for p in range(2):
+                halo_up(p).start()
+
 
     def energy_of(i):
         return lax.rem(i + en, energy_count)
-
-    def swap(i, p, parity):
-        return remote(blocks.at[parity, i, p], blocks.at[parity, i, p], block_send.at[i, p],
-                      block_recv.at[i, p], "kz", sibling)
 
     def load_block(i, p):
         e = energy_of(i)
@@ -147,15 +158,23 @@
         def _():
             blocks[odd, i, p] = below + above
 
-        @pl.when(e == 0)
-        def _():
-            pl.when(en > 0)(lambda: halo_up(p).wait_recv())
+        @pl.when((e == 0) & (en > 0))
+        def _():
+            halo_up(p).wait_recv()
             blocks[odd, i, p] = halo[0, p] + above
 
-        @pl.when((e > 0) & (e == energy_count - 1))
-        def _():
-            pl.when(en < en_count - 1)(lambda: halo_down(p).wait_recv())
+        @pl.when((e == 0) & (en == 0))
+        def _():
+            blocks[odd, i, p] = above
+
+        @pl.when((e > 0) & (e == energy_count - 1) & (en < en_count - 1))
+        def _():
+            halo_down(p).wait_recv()
             blocks[odd, i, p] = below + halo[1, p]
+
+        @pl.when((e > 0) & (e == energy_count - 1) & (en == en_count - 1))
+        def _():
+            blocks[odd, i, p] = below
 
         swap(i, p, odd).start()
 
@@ -173,20 +192,22 @@
 
     def over(i, p, j, side):
         d, t = messages[j]
-        return remote(message.at[i, p, j],
+        return remote(message.at[i, t, p, d],
                       arrived.at[d, i, p, pl.ds(pl.multiple_of(side * half, half), half)],
-                      kz_send.at[i, p, j], kz_recv.at[d, i, p, side], "kz", far(d, t))
+                      kz_send.at[i, t], kz_recv.at[i], "kz", far(d, t))
 
     def near_half(i, p, parity, side):
         at = near.at[parity, i, p, pl.ds(pl.multiple_of(side * half, half), half)]
-        return remote(at, at, near_send.at[i, p], near_recv.at[i, p], "kz", sibling)
-
-    def block_terms(i, p):
+        return remote(at, at, near_send, near_recv.at[i], "kz", sibling)
+
+    def block_terms(i, p, between=lambda: None):
+        between()
         swap(i, p, 1 - odd).wait_recv()
         first = [
             dot_split((left3[:, :n], left3[:, 2 * n:]), split(blocks[source, i, p]))
             for source in range(2)
         ]
+        between()
         for m in range(modes):
             at = slice(m * half, (m + 1) * half)
             high, low = split(jnp.concatenate([first[0][at], first[1][at]], axis=0))
@@ -194,15 +215,14 @@
                 jnp.concatenate([high, high, low], axis=1), right3[m],
                 preferred_element_type=jnp.float32,
             )
+            between()
 
     def block_messages(i, p):
         for j, (d, t) in enumerate(messages):
-            message[i, p, j] = sum(
+            message[i, t, p, d] = sum(
                 picked(mode_far.at[2 * d + t], column, source)
                 for source in range(2) for column in columns(d, t, source)
             )
-            if t == 0:
-                over(i, p, j, odd).start()
         at = pl.ds(pl.multiple_of(odd * half, half), half)
         for t in range(2):
             near[t, i, p, at] = (
@@ -211,18 +231,21 @@
             )
         near_half(i, p, 1 - odd, odd).start()
 
-    def send_odds(i):
-        for p in range(2):
-            for j, (d, t) in enumerate(messages):
-                if t == 1:
-                    over(i, p, j, odd).start()
+    def targets(side):
+        return [j for j, (d, t) in enumerate(messages) if t == side]
+
+    def send(i, p, side):
+        for j in targets(side):
+            over(i, p, j, odd).start()
+
+    def drain(i, side):
+        whole = message.at[i, side]
+        remote(whole, whole, kz_send.at[i, side], kz_recv.at[i], "kz",
+               far(0, side)).wait_send()
 
     def collect(i, p):
-        near_half(i, p, odd, 1 - odd).wait_recv()
         value = near[odd, i, p]
         for d in range(len(steps)):
-            for side in range(2):
-                over(i, p, 2 * d, side).wait_recv()
             value = value + arrived[d, i, p]
         return value
 
@@ -234,7 +257,7 @@
     def link(i, j):
         p, at = place(j)
         return remote(out_ref.at[energy_of(i), p, at], before.at[i, p, at],
-                      sp_send.at[i, j], sp_recv.at[i, j], "sp", sp + 1)
+                      sp_send.at[i], sp_recv.at[i, j], "sp", sp + 1)
 
     def chain_step(i, j):
         p, at = place(j)
@@ -252,6 +275,8 @@
         @pl.when(sp < sp_count - 1)
         def _():
             link(i, j).start()
+
+    early = jnp.clip(pieces - (sp - 1) * (ROW_BLOCKS - 1), 0, pieces)
 
     def chain_part(i, first, last):
         @pl.loop(first, last)
@@ -259,6 +284,10 @@
             chain_step(i, j)
 
     def invert(i):
+        whole = near.at[odd, i, :, pl.ds(pl.multiple_of((1 - odd) * half, half), half)]
+        remote(whole, whole, near_send, near_recv.at[i], "kz", sibling).wait_recv()
+        whole = arrived.at[:, i]
+        remote(whole, whole, kz_send.at[i, 0], kz_recv.at[i], "kz", far(0, 0)).wait_recv()
         e = energy_of(i)
         guess = guess_ref[e]
         shift = onsite_ref[...] - energy_ref[e]
@@ -272,20 +301,27 @@
                 jnp.concatenate([a, b], axis=0) for a, b in zip(split(re), split(im))
             )
 
-        def left(re, im):
-            return tuple(complex_pair(a, b) for a, b in zip(split(re), split(im)))
-
-        r_left = left(r_re, r_im)
-        square = dot_split(r_left, stack(r_re, r_im))
-        s_re, s_im = square[:n], square[n:]
-        s_stack = stack(s_re, s_im)
-        cube = dot_split(r_left, s_stack)
-        fourth = dot_split(left(s_re, s_im), s_stack)
+        def sides(re, im):
+            return split(re), split(im), split(re + im)
+
+        def joined(first, second):
+            return tuple(jnp.concatenate(pair, axis=0) for pair in zip(first, second))
+
+        def finish(products):
+            re, im, both = products
+            return re - im, both - re - im
+
+        r_sides = sides(r_re, r_im)
+        s_re, s_im = finish([dot_split(side, side) for side in r_sides])
+        s_sides = sides(s_re, s_im)
+        products = [dot_split(joined(r, s), s) for r, s in zip(r_sides, s_sides)]
+        cube = finish([product[:n] for product in products])
+        fourth = finish([product[n:] for product in products])
         one = jnp.where(diagonal, 1.0, 0.0)
-        p_re = one + r_re + s_re + cube[:n]
-        p_im = r_im + s_im + cube[n:]
+        p_re = one + r_re + s_re + cube[0]
+        p_im = r_im + s_im + cube[1]
         re, im = split(p_re), split(p_im)
-        fourth = stack(fourth[:n], fourth[n:])
+        fourth = stack(*fourth)
         for block in range(2):
             at = slice(block * half, (block + 1) * half)
             rows_left = tuple(complex_pair(a[at], b[at]) for a, b in zip(re, im))
@@ -294,12 +330,11 @@
             inverse[i, 1, at] = guess * (p_im[at] + result[half:])
             pl.when(sp == 0)(lambda: chain_part(i, block * ROW_BLOCKS, (block + 1) * ROW_BLOCKS))
 
-    for e in range(energy_count):
-        green_load(e, 0).wait()
-    load_block(0, 0)
-    for e in range(energy_count):
-        green_load(e, 1).wait()
-    load_block(0, 1)
+    if not direct:
+        start_up()
+        green_load.wait()
+        for p in range(2):
+            load_block(0, p)
     for load in small_loads:
         load.wait()
     coupling_load.wait()
@@ -310,53 +345,108 @@
         left3[at] = jnp.concatenate([high, high, low], axis=1)
         high, low = split(coupling_ref[m].T * weight_ref[m])
         right3[m] = jnp.concatenate([high, low, high], axis=0)
+    if direct:
+        start_up()
+        for p in range(2):
+            first_load(p).wait()
     block_terms(0, 0)
     mode_to_sibling(1 - odd).wait_recv()
     for d, t in messages:
         mode_to_origin(d, t, t).wait_recv()
     block_messages(0, 0)
+    send(0, 0, 0)
     block_terms(0, 1)
     block_messages(0, 1)
-    send_odds(0)
+    send(0, 1, 0)
     across = jnp.broadcast_to(hopping_ref[...], (n, n))
     outer[...] = across * across.T
+
+    @pl.when(sp < sp_count - 1)
+    def _():
+        pl.semaphore_wait(ready.at[1], 1)
+
+    if direct:
+        green_load.wait()
+    if energy_count > 1:
+        load_block(1, 0)
+    drain(0, 0)
+    for p in range(2):
+        send(0, p, 1)
+
     for i in range(energy_count):
         last = i == energy_count - 1
 
-        def second(i=i):
+        def second(i=i, between=lambda: None):
             load_block(i + 1, 1)
-            block_terms(i + 1, 1)
+            between()
+            drain(i, 1)
+            send(i + 1, 0, 0)
+            block_terms(i + 1, 1, between)
             block_messages(i + 1, 1)
-            send_odds(i + 1)
-
-        if not last:
+            send(i + 1, 1, 0)
+
+        def turn(i=i):
+            drain(i + 1, 0)
+            for p in range(2):
+                send(i + 1, p, 1)
+
+        if last:
+            invert(i)
+            drain(i, 1)
+            pl.when(sp > 0)(lambda i=i: chain_part(i, 0, pieces))
+            continue
+        if i > 0:
             load_block(i + 1, 0)
-            block_terms(i + 1, 0)
-            block_messages(i + 1, 0)
-            pl.when(odd == 1)(second)
+        block_terms(i + 1, 0)
+        block_messages(i + 1, 0)
+        pl.when(odd == 1)(second)
         invert(i)
-        if not last:
-            pl.when(odd == 0)(second)
-        pl.when(sp > 0)(lambda i=i: chain_part(i, 0, pieces))
+
+        @pl.when(odd == 0)
+        def _():
+            taken = []
+
+            def between():
+                step = len(taken)
+                taken.append(TAKEN[step] if step < len(TAKEN) else 0)
+                first, end = sum(taken[:step]), sum(taken)
+                if first < end:
+                    pl.when(sp == 1)(lambda: chain_part(i, first, end))
+
+            second(between=between)
+            begun = jnp.where(sp == 1, sum(taken), 0)
+            pl.when(sp > 0)(lambda: chain_part(i, begun, early))
+            turn()
+            pl.when(sp > 0)(lambda: chain_part(i, early, pieces))
+
+        @pl.when(odd == 1)
+        def _():
+            turn()
+            pl.when(sp > 0)(lambda: chain_part(i, 0, pieces))
 
     mode_to_sibling(odd).wait_send()
     for d, t in messages:
         mode_to_origin(d, t, odd).wait_send()
-    for p in range(2):
-        pl.when(en < en_count - 1)(lambda p=p: halo_up(p).wait_send())
-        pl.when(en > 0)(lambda p=p: halo_down(p).wait_send())
-    for i in range(energy_count):
-        for p in range(2):
-            swap(i, p, odd).wait_send()
-            near_half(i, p, 1 - odd, odd).wait_send()
-            for j in range(len(messages)):
-                over(i, p, j, odd).wait_send()
-
-        @pl.when(sp < sp_count - 1)
-        def _():
-            @pl.loop(0, pieces)
-            def _(j):
-                link(i, j).wait_send()
+    @pl.when(en < en_count - 1)
+    def _():
+        remote(green_in.at[energy_count - 1], halo.at[0], halo_send.at[0], halo_recv.at[0, 0],
+               "en", en + 1).wait_send()
+
+    @pl.when(en > 0)
+    def _():
+        remote(green_in.at[0], halo.at[1], halo_send.at[1], halo_recv.at[1, 0],
+               "en", en - 1).wait_send()
+
+    whole = blocks.at[odd]
+    remote(whole, whole, block_send, block_recv.at[0, 0], "kz", sibling).wait_send()
+    whole = near.at[1 - odd, :, :, pl.ds(pl.multiple_of(odd * half, half), half)]
+    remote(whole, whole, near_send, near_recv.at[0], "kz", sibling).wait_send()
+
+    @pl.when(sp < sp_count - 1)
+    def _():
+        for i in range(energy_count):
+            remote(out_ref.at[energy_of(i)], before.at[i], sp_send.at[i], sp_recv.at[i, 0],
+                   "sp", sp + 1).wait_send()
 
 
 def body(sizes, green, coupling, phonon_weight, mode_index, onsite, hopping, energies, guess_scale):
@@ -364,7 +454,7 @@
     modes = coupling.shape[1]
     blocks = (energy_count, 2, n, n)
     steps = 2 if sizes[0] > 2 * REACH else 1
-    halves = (energy_count, 2, 2 * steps, n // 2, n)
+    halves = (energy_count, 2, 2, steps, n // 2, n)
     pieces = 2 * ROW_BLOCKS
     hbm = pl.BlockSpec(memory_space=pltpu.HBM)
     vmem = pl.BlockSpec(memory_space=pltpu.VMEM)
@@ -396,20 +486,22 @@
             pltpu.VMEM(blocks, jnp.float32),
             pltpu.VMEM(blocks, jnp.float32),
             pltpu.VMEM((n, n), jnp.float32),
+            pltpu.SemaphoreType.REGULAR((2,)),
             dma((6,)),
             dma,
-            dma((energy_count, 2)),
+            dma,
+            dma((2,)),
             dma((2 * steps + 1,)),
             dma((2 * steps + 1,)),
+            dma((2,)),
             dma((2, 2)),
-            dma((2, 2)),
+            dma,
             dma((energy_count, 2)),
+            dma,
+            dma((energy_count,)),
             dma((energy_count, 2)),
-            dma((energy_count, 2)),
-            dma((energy_count, 2)),
-            dma((energy_count, 2, 2 * steps)),
-            dma((steps, energy_count, 2, 2)),
-            dma((energy_count, pieces)),
+            dma((energy_count,)),
+            dma((energy_count,)),
             dma((energy_count, pieces)),
         ],
         compiler_params=pltpu.CompilerParams(

time: 46.4 us -> 45.4 us (0.978)
  Pallas kernels: 45.3 us -> 44.3 us
    pallas_call x1, Pallas kernels: 45.3 us -> 44.3 us  [body(): pl.pallas_call(functools.partial(kernel, sizes), out_shape=jax.ShapeDtype...]
where the time goes in v3:
time: 45.4 us; the launch traced here: 45.2 us
  Pallas kernels  44.3 us (98%)
  local copies, waits for them, and re-layouts  0.97 us (2%)
    pallas_call x1, Pallas kernels, body(): pl.pallas_call(functools.partial(kernel, sizes), out_shape=jax.ShapeDtype...  44.3 us
    unnamed x1, local copies, waits for them, and re-layouts  0.97 us

profile of v3, /device:TPU:29, one launch (start us, length us, event | category | flops | bytes accessed | tf_op | source)
XLA Modules:
  0.0 45.2 jit_solution(10735138723023193573)
XLA Ops:
  0.0 44.3 %shard_map.82 = f32[2,2,256,256]{3,2,1,0:T(8,128)S(1)} custom-call(s32[5]{0:T(128)} %bitcast.10, f32[3]{0:T(128)} %weight_in.1, f32[2]{0:T(128)} %energy_in.1, f32[2]{0:T(128)} %bitcast.11, f32[2,2,256,256]{3,2,1,0:T(8,128)} %bitcast.8, f32[3,256,256]{2,1,0:T(8,128)} %bitcast.9, f32[1,256]{1,0:T(1,128)} %onsite_in.1, f32[1,256]{1,0:T(1,128)} %hopping_in.1), custom_call_target="tpu_custom_call" | custom-call | tf_op jit(solution)/shard_map/pallas_call | solution.py:463
  44.3 1.0 %copy.11 = f32[1,2,1,2,256,256]{5,4,3,2,1,0:T(8,128)} copy(f32[1,2,1,2,256,256]{5,4,3,2,1,0:T(8,128)S(1)} %bitcast.7) | data formatting | bytes 2097152

commit v4 on v3

--- a/solution.py
+++ b/solution.py
@@ -9,7 +9,7 @@
 
 REACH = 2
 ROW_BLOCKS = 8
-TAKEN = (1, 1, 2, 0, 1, 0)
+TAKEN = (1, 1, 2, 1, 0, 1)
 MESH = pl.DeviceIdType.MESH
 
 
@@ -188,7 +188,8 @@
         return ()
 
     def picked(row, column, source):
-        return terms[row[column], pl.ds(source * half, half)]
+        other = 1 - odd if source else odd
+        return terms[row[column], pl.ds(pl.multiple_of(other * half, half), half)]
 
     def over(i, p, j, side):
         d, t = messages[j]
@@ -200,13 +201,20 @@
         at = near.at[parity, i, p, pl.ds(pl.multiple_of(side * half, half), half)]
         return remote(at, at, near_send, near_recv.at[i], "kz", sibling)
 
-    def block_terms(i, p, between=lambda: None):
-        between()
-        swap(i, p, 1 - odd).wait_recv()
-        first = [
-            dot_split((left3[:, :n], left3[:, 2 * n:]), split(blocks[source, i, p]))
-            for source in range(2)
-        ]
+    def block_terms(i, p, between=lambda: None, gate=None):
+        def product(parity):
+            return dot_split((left3[:, :n], left3[:, 2 * n:]), split(blocks[parity, i, p]))
+
+        if gate is None:
+            swap(i, p, 1 - odd).wait_recv()
+            first = [product(odd), product(1 - odd)]
+        else:
+            first = [product(odd)]
+            between()
+            gate()
+            between()
+            swap(i, p, 1 - odd).wait_recv()
+            first.append(product(1 - odd))
         between()
         for m in range(modes):
             at = slice(m * half, (m + 1) * half)
@@ -378,10 +386,12 @@
 
         def second(i=i, between=lambda: None):
             load_block(i + 1, 1)
-            between()
-            drain(i, 1)
-            send(i + 1, 0, 0)
-            block_terms(i + 1, 1, between)
+
+            def gate():
+                drain(i, 1)
+                send(i + 1, 0, 0)
+
+            block_terms(i + 1, 1, between, gate)
             block_messages(i + 1, 1)
             send(i + 1, 1, 0)
 

time: 45.4 us -> 44.9 us (0.989)
  Pallas kernels: 44.3 us -> 43.8 us
where the time goes in v4:
time: 44.9 us; the launch traced here: 44.8 us
  Pallas kernels  43.8 us (98%)
  local copies, waits for them, and re-layouts  0.97 us (2%)
    pallas_call x1, Pallas kernels, body(): pl.pallas_call(functools.partial(kernel, sizes), out_shape=jax.ShapeDtype...  43.8 us
    unnamed x1, local copies, waits for them, and re-layouts  0.97 us

profile of v4, /device:TPU:29, one launch (start us, length us, event | category | flops | bytes accessed | tf_op | source)
XLA Modules:
  0.0 44.8 jit_solution(3793160126830920314)
XLA Ops:
  0.0 43.8 %shard_map.82 = f32[2,2,256,256]{3,2,1,0:T(8,128)S(1)} custom-call(s32[5]{0:T(128)} %bitcast.10, f32[3]{0:T(128)} %weight_in.1, f32[2]{0:T(128)} %energy_in.1, f32[2]{0:T(128)} %bitcast.11, f32[2,2,256,256]{3,2,1,0:T(8,128)} %bitcast.8, f32[3,256,256]{2,1,0:T(8,128)} %bitcast.9, f32[1,256]{1,0:T(1,128)} %onsite_in.1, f32[1,256]{1,0:T(1,128)} %hopping_in.1), custom_call_target="tpu_custom_call" | custom-call | tf_op jit(solution)/shard_map/pallas_call | solution.py:473
  43.8 1.0 %copy.11 = f32[1,2,1,2,256,256]{5,4,3,2,1,0:T(8,128)} copy(f32[1,2,1,2,256,256]{5,4,3,2,1,0:T(8,128)S(1)} %bitcast.7) | data formatting | bytes 2097152

commit v5 on v4

--- a/solution.py
+++ b/solution.py
@@ -9,6 +9,8 @@
 
 REACH = 2
 ROW_BLOCKS = 8
+PARTS = 4
+CUTS = ((0, 1), (1, 4))
 TAKEN = (1, 1, 2, 1, 0, 1)
 MESH = pl.DeviceIdType.MESH
 
@@ -129,9 +131,9 @@
         return remote(source, blocks.at[parity, i, p], block_send, block_recv.at[i, p],
                       "kz", sibling)
 
-    mode_to_sibling(odd).start()
     for d, t in messages:
         mode_to_origin(d, t, odd).start()
+    mode_to_sibling(odd).start()
     if direct:
         for p in range(2):
             swap(0, p, odd).start()
@@ -225,12 +227,17 @@
             )
             between()
 
-    def block_messages(i, p):
-        for j, (d, t) in enumerate(messages):
-            message[i, t, p, d] = sum(
-                picked(mode_far.at[2 * d + t], column, source)
-                for source in range(2) for column in columns(d, t, source)
-            )
+    def form(i, p, side):
+        for d, t in messages:
+            if t == side:
+                message[i, t, p, d] = sum(
+                    picked(mode_far.at[2 * d + t], column, source)
+                    for source in range(2) for column in columns(d, t, source)
+                )
+
+    def block_messages(i, p, sides=(0, 1)):
+        for side in sides:
+            form(i, p, side)
         at = pl.ds(pl.multiple_of(odd * half, half), half)
         for t in range(2):
             near[t, i, p, at] = (
@@ -258,9 +265,10 @@
         return value
 
     def place(j):
-        block, rest = j // ROW_BLOCKS, lax.rem(j, ROW_BLOCKS)
-        p, r = rest // (ROW_BLOCKS // 2), lax.rem(rest, ROW_BLOCKS // 2)
-        return p, pl.ds(pl.multiple_of(block * half + r * rows, rows), rows)
+        group = pieces // PARTS
+        block, rest = j // group, lax.rem(j, group)
+        p, r = rest // (group // 2), lax.rem(rest, group // 2)
+        return p, pl.ds(pl.multiple_of(block * (n // PARTS) + r * rows, rows), rows)
 
     def link(i, j):
         p, at = place(j)
@@ -312,9 +320,6 @@
         def sides(re, im):
             return split(re), split(im), split(re + im)
 
-        def joined(first, second):
-            return tuple(jnp.concatenate(pair, axis=0) for pair in zip(first, second))
-
         def finish(products):
             re, im, both = products
             return re - im, both - re - im
@@ -322,21 +327,23 @@
         r_sides = sides(r_re, r_im)
         s_re, s_im = finish([dot_split(side, side) for side in r_sides])
         s_sides = sides(s_re, s_im)
-        products = [dot_split(joined(r, s), s) for r, s in zip(r_sides, s_sides)]
-        cube = finish([product[:n] for product in products])
-        fourth = finish([product[n:] for product in products])
         one = jnp.where(diagonal, 1.0, 0.0)
-        p_re = one + r_re + s_re + cube[0]
-        p_im = r_im + s_im + cube[1]
-        re, im = split(p_re), split(p_im)
-        fourth = stack(*fourth)
-        for block in range(2):
-            at = slice(block * half, (block + 1) * half)
-            rows_left = tuple(complex_pair(a[at], b[at]) for a, b in zip(re, im))
+        s_stack = stack(s_re, s_im)
+        fourth = stack(*finish([dot_split(side, side) for side in s_sides]))
+        q_re, q_im = one + r_re + s_re, r_im + s_im
+        for first, last in CUTS:
+            at = slice(first * n // PARTS, last * n // PARTS)
+            size = (last - first) * n // PARTS
+            rows_left = tuple(complex_pair(a[at], b[at]) for a, b in zip(*r_sides[:2]))
+            cube = dot_split(rows_left, s_stack)
+            p_re, p_im = q_re[at] + cube[:size], q_im[at] + cube[size:]
+            rows_left = tuple(complex_pair(a, b) for a, b in zip(split(p_re), split(p_im)))
             result = dot_split(rows_left, fourth)
-            inverse[i, 0, at] = guess * (p_re[at] + result[:half])
-            inverse[i, 1, at] = guess * (p_im[at] + result[half:])
-            pl.when(sp == 0)(lambda: chain_part(i, block * ROW_BLOCKS, (block + 1) * ROW_BLOCKS))
+            inverse[i, 0, at] = guess * (p_re + result[:size])
+            inverse[i, 1, at] = guess * (p_im + result[size:])
+            pl.when(sp == 0)(
+                lambda: chain_part(i, first * pieces // PARTS, last * pieces // PARTS)
+            )
 
     if not direct:
         start_up()
@@ -358,11 +365,15 @@
         for p in range(2):
             first_load(p).wait()
     block_terms(0, 0)
+    for side in range(2):
+        for d, t in messages:
+            if t == side:
+                mode_to_origin(d, t, t).wait_recv()
+        if side == 0:
+            form(0, 0, 0)
+            send(0, 0, 0)
     mode_to_sibling(1 - odd).wait_recv()
-    for d, t in messages:
-        mode_to_origin(d, t, t).wait_recv()
-    block_messages(0, 0)
-    send(0, 0, 0)
+    block_messages(0, 0, (1,))
     block_terms(0, 1)
     block_messages(0, 1)
     send(0, 1, 0)

time: 44.9 us -> 44.8 us (level)
  no operation moved by 1% of the time
where the time goes in v5:
time: 44.8 us; the launch traced here: 44.7 us
  Pallas kernels  43.7 us (98%)
  local copies, waits for them, and re-layouts  0.97 us (2%)
    pallas_call x1, Pallas kernels, body(): pl.pallas_call(functools.partial(kernel, sizes), out_shape=jax.ShapeDtype...  43.7 us
    unnamed x1, local copies, waits for them, and re-layouts  0.97 us

profile of v5, /device:TPU:29, one launch (start us, length us, event | category | flops | bytes accessed | tf_op | source)
XLA Modules:
  0.0 44.7 jit_solution(14247411681321015447)
XLA Ops:
  0.0 43.7 %shard_map.82 = f32[2,2,256,256]{3,2,1,0:T(8,128)S(1)} custom-call(s32[5]{0:T(128)} %bitcast.10, f32[3]{0:T(128)} %weight_in.1, f32[2]{0:T(128)} %energy_in.1, f32[2]{0:T(128)} %bitcast.11, f32[2,2,256,256]{3,2,1,0:T(8,128)} %bitcast.8, f32[3,256,256]{2,1,0:T(8,128)} %bitcast.9, f32[1,256]{1,0:T(1,128)} %onsite_in.1, f32[1,256]{1,0:T(1,128)} %hopping_in.1), custom_call_target="tpu_custom_call" | custom-call | tf_op jit(solution)/shard_map/pallas_call | solution.py:484
  43.7 1.0 %copy.11 = f32[1,2,1,2,256,256]{5,4,3,2,1,0:T(8,128)} copy(f32[1,2,1,2,256,256]{5,4,3,2,1,0:T(8,128)S(1)} %bitcast.7) | data formatting | bytes 2097152

commit v6 on v5

--- a/solution.py
+++ b/solution.py
@@ -11,7 +11,7 @@
 ROW_BLOCKS = 8
 PARTS = 4
 CUTS = ((0, 1), (1, 4))
-TAKEN = (1, 1, 2, 1, 0, 1)
+TAKEN = (2, 1, 1, 1, 0, 1)
 MESH = pl.DeviceIdType.MESH
 
 
@@ -413,8 +413,8 @@
 
         if last:
             invert(i)
+            pl.when(sp > 0)(lambda i=i: chain_part(i, 0, pieces))
             drain(i, 1)
-            pl.when(sp > 0)(lambda i=i: chain_part(i, 0, pieces))
             continue
         if i > 0:
             load_block(i + 1, 0)

time: 44.8 us -> 44.8 us (level)
  no operation moved by 1% of the time
where the time goes in v6:
time: 44.8 us; the launch traced here: 44.6 us
  Pallas kernels  43.7 us (98%)
  local copies, waits for them, and re-layouts  0.97 us (2%)
    pallas_call x1, Pallas kernels, body(): pl.pallas_call(functools.partial(kernel, sizes), out_shape=jax.ShapeDtype...  43.7 us
    unnamed x1, local copies, waits for them, and re-layouts  0.97 us

profile of v6, /device:TPU:29, one launch (start us, length us, event | category | flops | bytes accessed | tf_op | source)
XLA Modules:
  0.0 44.6 jit_solution(997206642693298540)
XLA Ops:
  0.0 43.7 %shard_map.82 = f32[2,2,256,256]{3,2,1,0:T(8,128)S(1)} custom-call(s32[5]{0:T(128)} %bitcast.10, f32[3]{0:T(128)} %weight_in.1, f32[2]{0:T(128)} %energy_in.1, f32[2]{0:T(128)} %bitcast.11, f32[2,2,256,256]{3,2,1,0:T(8,128)} %bitcast.8, f32[3,256,256]{2,1,0:T(8,128)} %bitcast.9, f32[1,256]{1,0:T(1,128)} %onsite_in.1, f32[1,256]{1,0:T(1,128)} %hopping_in.1), custom_call_target="tpu_custom_call" | custom-call | tf_op jit(solution)/shard_map/pallas_call | solution.py:484
  43.7 1.0 %copy.11 = f32[1,2,1,2,256,256]{5,4,3,2,1,0:T(8,128)} copy(f32[1,2,1,2,256,256]{5,4,3,2,1,0:T(8,128)S(1)} %bitcast.7) | data formatting | bytes 2097152

commit v7 on v6

--- a/solution.py
+++ b/solution.py
@@ -11,7 +11,7 @@
 ROW_BLOCKS = 8
 PARTS = 4
 CUTS = ((0, 1), (1, 4))
-TAKEN = (2, 1, 1, 1, 0, 1)
+TAKEN = (1, 1, 2, 1, 0, 1)
 MESH = pl.DeviceIdType.MESH
 
 
@@ -64,9 +64,8 @@
 
     direct = en_count == 2 and energy_count == 2
 
-    def first_load(p):
-        return pltpu.make_async_copy(green_in.at[1 - en, p], blocks.at[odd, 0, p],
-                                     first_sem.at[p])
+    def first_load():
+        return pltpu.make_async_copy(green_in.at[1 - en], blocks.at[odd, 0], first_sem)
 
     green_load = pltpu.make_async_copy(green_in, green_ref, green_sem)
     coupling_load = pltpu.make_async_copy(coupling_in, coupling_ref, coupling_sem)
@@ -89,8 +88,7 @@
         pl.when(here < count - 1)(lambda axis=axis, here=here: greet(axis, here + 1))
     coupling_load.start()
     if direct:
-        for p in range(2):
-            first_load(p).start()
+        first_load().start()
     for load in small_loads:
         load.start()
     green_load.start()
@@ -362,8 +360,7 @@
         right3[m] = jnp.concatenate([high, low, high], axis=0)
     if direct:
         start_up()
-        for p in range(2):
-            first_load(p).wait()
+        first_load().wait()
     block_terms(0, 0)
     for side in range(2):
         for d, t in messages:
@@ -511,7 +508,7 @@
             dma((6,)),
             dma,
             dma,
-            dma((2,)),
+            dma,
             dma((2 * steps + 1,)),
             dma((2 * steps + 1,)),
             dma((2,)),

time: 44.8 us -> 44.8 us (level)
  no operation moved by 1% of the time
where the time goes in v7:
time: 44.8 us; the launch traced here: 44.7 us
  Pallas kernels  43.7 us (98%)
  local copies, waits for them, and re-layouts  0.97 us (2%)
    pallas_call x1, Pallas kernels, body(): pl.pallas_call(functools.partial(kernel, sizes), out_shape=jax.ShapeDtype...  43.7 us
    unnamed x1, local copies, waits for them, and re-layouts  0.97 us

profile of v7, /device:TPU:29, one launch (start us, length us, event | category | flops | bytes accessed | tf_op | source)
XLA Modules:
  0.0 44.7 jit_solution(2011814144590301734)
XLA Ops:
  0.0 43.7 %shard_map.82 = f32[2,2,256,256]{3,2,1,0:T(8,128)S(1)} custom-call(s32[5]{0:T(128)} %bitcast.10, f32[3]{0:T(128)} %weight_in.1, f32[2]{0:T(128)} %energy_in.1, f32[2]{0:T(128)} %bitcast.11, f32[2,2,256,256]{3,2,1,0:T(8,128)} %bitcast.8, f32[3,256,256]{2,1,0:T(8,128)} %bitcast.9, f32[1,256]{1,0:T(1,128)} %onsite_in.1, f32[1,256]{1,0:T(1,128)} %hopping_in.1), custom_call_target="tpu_custom_call" | custom-call | tf_op jit(solution)/shard_map/pallas_call | solution.py:481
  43.7 1.0 %copy.11 = f32[1,2,1,2,256,256]{5,4,3,2,1,0:T(8,128)} copy(f32[1,2,1,2,256,256]{5,4,3,2,1,0:T(8,128)S(1)} %bitcast.7) | data formatting | bytes 2097152
